TPU v7x, 128 devices: a whole 4x4x4 slice. The times are simulated.
128 devices in a mesh: section: 8 (over z_lo, y), dp: 16 (over z_hi, x, core).
Axes of the slice: x: 4, y: 4, z: 4 (z_hi: 2, z_lo: 2; z = z_hi * 2 + z_lo), core: 2. Of those that a mesh axis runs over, the one named last changes fastest.
Arguments:
- enc_in: bfloat16 [8, 2, 8192, 1152], P('section', None, 'dp'), may hold values from -6 to 6
- dec_in: bfloat16 [8, 2, 8192, 1152], P('section', None, 'dp'), may hold values from -6 to 6
- cotangent: bfloat16 [8, 2, 8192, 1152], P('section', None, 'dp'), may hold values from -0.23925781 to 0.23925781
- w_proj: float32 [8, 1152, 1152], P('section', 'dp'), may hold values from -0.1875 to 0.1875
- w_skip: float32 [8, 2304, 1152], P('section', 'dp'), may hold values from -0.125 to 0.125
- m_proj: float32 [8, 1152, 1152], P('section', 'dp'), may hold values from -3 to 3
- v_proj: float32 [8, 1152, 1152], P('section', 'dp'), may hold values from 0.05 to 1
- m_skip: float32 [8, 2304, 1152], P('section', 'dp'), may hold values from -3 to 3
- v_skip: float32 [8, 2304, 1152], P('section', 'dp'), may hold values from 0.05 to 1
Outputs:
- dec_out: bfloat16 [8, 2, 8192, 1152], P('section', None, 'dp')
- enc_grad: bfloat16 [8, 2, 8192, 1152], P('section', None, 'dp')
- dec_grad: bfloat16 [8, 2, 8192, 1152], P('section', None, 'dp')
- new_w_proj: float32 [8, 1152, 1152], P('section', 'dp')
- new_m_proj: float32 [8, 1152, 1152], P('section', 'dp')
- new_v_proj: float32 [8, 1152, 1152], P('section', 'dp')
- new_w_skip: float32 [8, 2304, 1152], P('section', 'dp')
- new_m_skip: float32 [8, 2304, 1152], P('section', 'dp')
- new_v_skip: float32 [8, 2304, 1152], P('section', 'dp')
All inputs are finite; a program needn't handle non-finite values.
Results may differ from a plain program's by a relative error of at most 0.025.
Values may be sent and summed in bfloat16 or wider, within the bound.
A program may use at most 128 MiB of HBM per device.

v0:
```python
import jax
import jax.numpy as jnp
from jax import lax
from jax.sharding import PartitionSpec as P

half_root = 0.7071067811865476
gauss_norm = 0.3989422804014327
beta_one = 0.9
beta_two = 0.95
learn_rate = 0.002
adam_eps = 1e-08
correct_one = 1.0 - 0.9**10
correct_two = 1.0 - 0.95**10


def swapped(value, axis, bit):
    mask = 2**bit
    pairs = [(source, source ^ mask) for source in range(lax.axis_size(axis))]
    return lax.ppermute(value, axis, pairs)


def in_blocks(value, dim, count):
    before, after = (value.shape[:dim], value.shape[dim + 1 :])
    return jnp.moveaxis(value.reshape(*before, count, -1, *after), dim, 0)


def one_scatter(arrays, axis, dims):
    count = lax.axis_size(axis)
    pieces = [in_blocks(a, dim, count) for a, dim in zip(arrays, dims)]
    lines = jnp.concatenate([b.reshape(count, -1) for b in pieces], axis=1)
    span = max(16, -(-lines.shape[1] // 1024) * 8)
    lines = jnp.pad(lines, ((0, 0), (0, span * 128 - lines.shape[1]))).reshape(-1, 128)
    ravelled, at, outs = (lax.psum_scatter(lines, axis, tiled=True).reshape(-1), 0, [])
    for b in pieces:
        part = b[0]
        outs.append(ravelled[at : at + part.size].reshape(part.shape))
        at += part.size
    return tuple(outs)


def gelu_parts(preact):
    normal_cdf = 0.5 * (1.0 + lax.erf(preact * half_root))
    density = jnp.exp(-0.5 * preact * preact) * gauss_norm
    return (preact * normal_cdf, normal_cdf + preact * density)


def adam_update(weight, moment, second, grad):
    new_moment = beta_one * moment + (1.0 - beta_one) * grad
    new_second = beta_two * second + (1.0 - beta_two) * grad * grad
    step_size = new_moment / correct_one / (jnp.sqrt(new_second / correct_two) + adam_eps)
    return (weight - learn_rate * step_size, new_moment, new_second)


def top_bit():
    return lax.axis_size("section").bit_length() - 2


def send_forward(value):
    return swapped(value, "section", top_bit())


def send_backward(value):
    return swapped(value, "section", top_bit())


def layer_pass(enc_rows, dec_rows, out_grad, proj_full, skip_full):
    width = enc_rows.shape[1]
    skip_local = jnp.dot(enc_rows, proj_full, preferred_element_type=jnp.float32).astype(
        jnp.bfloat16
    )
    skip_remote = send_forward(skip_local)
    joined = jnp.concatenate([dec_rows, skip_remote], axis=1)
    preact = jnp.dot(joined, skip_full, preferred_element_type=jnp.float32)
    activated, gelu_slope = gelu_parts(preact)
    dec_out = activated.astype(jnp.bfloat16)
    pre_grad = (out_grad.astype(jnp.float32) * gelu_slope).astype(jnp.bfloat16)
    input_grad = jnp.einsum("rk,jk->rj", pre_grad, skip_full, preferred_element_type=jnp.float32)
    dec_grad = input_grad[:, :width].astype(jnp.bfloat16)
    skip_sent = input_grad[:, width:].astype(jnp.bfloat16)
    skip_grad = send_backward(skip_sent)
    enc_grad = jnp.einsum(
        "rk,jk->rj", skip_grad, proj_full, preferred_element_type=jnp.float32
    ).astype(jnp.bfloat16)
    grad_proj = jnp.einsum("rj,rk->jk", enc_rows, skip_grad, preferred_element_type=jnp.float32)
    grad_skip = jnp.einsum("rj,rk->jk", joined, pre_grad, preferred_element_type=jnp.float32)
    return (dec_out, enc_grad, dec_grad, grad_proj, grad_skip)


def body(enc_in, dec_in, cotangent, w_proj, w_skip, m_proj, v_proj, m_skip, v_skip):
    proj_all, skip_all = (
        lax.all_gather(w_proj.astype(jnp.bfloat16), "dp", axis=1, tiled=True),
        lax.all_gather(w_skip.astype(jnp.bfloat16), "dp", axis=1, tiled=True),
    )
    proj_full = proj_all[0]
    skip_full = skip_all[0]
    micro = enc_in.shape[1]
    tokens_here = enc_in.shape[2]
    width = enc_in.shape[3]
    rows = micro * tokens_here
    result = layer_pass(
        enc_in[0].reshape(rows, width),
        dec_in[0].reshape(rows, width),
        cotangent[0].reshape(rows, width),
        proj_full,
        skip_full,
    )
    dec_out = result[0].reshape(micro, tokens_here, width)
    enc_grad = result[1].reshape(micro, tokens_here, width)
    dec_grad = result[2].reshape(micro, tokens_here, width)
    proj_sum, skip_sum = tuple(
        (
            part.astype(jnp.float32)
            for part in one_scatter(
                (result[3].astype(jnp.bfloat16), result[4].astype(jnp.bfloat16)), "dp", (0, 0)
            )
        )
    )
    new_w_proj, new_m_proj, new_v_proj = adam_update(w_proj[0], m_proj[0], v_proj[0], proj_sum)
    new_w_skip, new_m_skip, new_v_skip = adam_update(w_skip[0], m_skip[0], v_skip[0], skip_sum)
    return (
        dec_out[None],
        enc_grad[None],
        dec_grad[None],
        new_w_proj[None],
        new_m_proj[None],
        new_v_proj[None],
        new_w_skip[None],
        new_m_skip[None],
        new_v_skip[None],
    )


def solution(mesh):
    in_specs = (
        P("section", None, "dp", None),
        P("section", None, "dp", None),
        P("section", None, "dp", None),
        P("section", "dp", None),
        P("section", "dp", None),
        P("section", "dp", None),
        P("section", "dp", None),
        P("section", "dp", None),
        P("section", "dp", None),
    )
    out_specs = (
        P("section", None, "dp", None),
        P("section", None, "dp", None),
        P("section", None, "dp", None),
        P("section", "dp", None),
        P("section", "dp", None),
        P("section", "dp", None),
        P("section", "dp", None),
        P("section", "dp", None),
        P("section", "dp", None),
    )
    return jax.shard_map(body, mesh=mesh, in_specs=in_specs, out_specs=out_specs, check_vma=False)
```

profile of v0, /device:TPU:0, one launch (start us, length us, event | category | flops | bytes accessed | tf_op | source)
XLA Modules:
  0.0 429.5 jit_solution(92079628465543061)
XLA Ops:
  7.2 1.8 convert_element_type.71
  9.1 1.9 convert_element_type.73
  11.1 52.7 %all-gather.3.cloned.1.call-done = bf16[1,1152,1152]{2,1,0:T(8,128)(2,1)} async-done(((bf16[1,72,1152]{2,1,0:T(8,128)(2,1)}), bf16[1,1152,1152]{2,1,0:T(8,128)(2,1)}) %all-gather.3.cloned.1.call-update) | async-done | bytes 2654224 | tf_op jit(solution)/shard_map/all_gather | solution.py:91
  63.7 5.4 %convolution_convert_fusion.4 = bf16[1024,1152]{1,0:T(8,128)(2,1)S(1)} fusion(bf16[1024,1152]{1,0:T(8,128)(2,1)S(1)} %bitcast.29, bf16[1,1152,1152]{2,1,0:T(8,128)(2,1)} %all-gather.3.cloned.1.call-done), kind=kOutput, calls=%fused_computation.19 | convolution fusion | flops 2719088640 | bytes 7372800 | tf_op jit(solution)/shard_map/dot_general | solution.py:68
  69.9 70.6 %collective-permute-done = bf16[1024,1152]{1,0:T(8,128)(2,1)} collective-permute-done((bf16[1024,1152]{1,0:T(8,128)(2,1)S(1)}, bf16[1024,1152]{1,0:T(8,128)(2,1)}, u32[]{:S(2)}, u32[]{:S(2)}) %collective-permute-start) | collective-permute-done | bytes 2359328 | tf_op jit(solution)/shard_map/ppermute | solution.py:19
  142.1 13.2 %fusion.9 = (bf16[1024,1152]{1,0:T(8,128)(2,1)S(1)}, bf16[1024,1152]{1,0:T(8,128)(2,1)}) fusion(bf16[1,2,512,1152]{3,2,1,0:T(8,128)(2,1)} %param.11, bf16[1,2304,1152]{2,1,0:T(8,128)(2,1)} %all-gather.5.cloned.1.call-done, bf16[1024,1152]{1,0:T(8,128)(2,1)} %collective-permute-done, bf16[1024,1152]{1,0:T(8,128)(2,1)} %bitcast.32), kind=kOutput, calls=%fused_computation.14 | convolution fusion | flops 5460590592 | bytes 17104896 | tf_op jit(solution)/shard_map/dot_general | solution.py:73
  155.3 6.5 %convolution_convert_fusion.2 = bf16[1024,2304]{1,0:T(8,128)(2,1)S(1)} fusion(bf16[1024,1152]{1,0:T(8,128)(2,1)S(1)} %get-tuple-element.17, bf16[1,2304,1152]{2,1,0:T(8,128)(2,1)S(1)} %copy-done.3), kind=kOutput, calls=%fused_computation.5 | convolution fusion | flops 5438177280 | bytes 12386304 | tf_op jit(solution)/shard_map/rk,jk->rj/dot_general | solution.py:77
  161.9 2.5 fusion.18
  165.1 8.4 %convolution_convert_fusion = bf16[2304,1152]{1,0:T(8,128)(2,1)} fusion(bf16[1024,1152]{1,0:T(8,128)(2,1)S(1)} %get-tuple-element.17, bf16[1024,1152]{1,0:T(8,128)(2,1)} %collective-permute-done, bf16[1024,1152]{1,0:T(8,128)(2,1)S(1)} %bitcast.33), kind=kOutput, calls=%fused_computation | convolution fusion | flops 5447909376 | bytes 12386304 | tf_op jit(solution)/shard_map/rj,rk->jk/dot_general | solution.py:85
  173.5 5.7 %reshape_reshape.7 = bf16[16,165888]{1,0:T(8,128)(2,1)} reshape(bf16[2304,1152]{1,0:T(8,128)(2,1)} %convolution_convert_fusion) | data formatting | bytes 10616832 | tf_op jit(solution)/shard_map/reshape;reshape | solution.py:30
  179.2 39.0 %collective-permute-done.1 = bf16[1024,1152]{1,0:T(8,128)(2,1)} collective-permute-done((bf16[1024,1152]{1,0:T(8,128)(2,1)}, bf16[1024,1152]{1,0:T(8,128)(2,1)}, u32[]{:S(2)}, u32[]{:S(2)}) %collective-permute-start.1) | collective-permute-done | bytes 2359328 | tf_op jit(solution)/shard_map/ppermute | solution.py:19
  218.1 6.4 %fusion = bf16[1152,1152]{0,1:T(8,128)(2,1)} fusion(bf16[1024,1152]{1,0:T(8,128)(2,1)} %collective-permute-done.1, bf16[1024,1152]{1,0:T(8,128)(2,1)S(1)} %bitcast.30), kind=kOutput, calls=%fused_computation.4 | convolution fusion | flops 2719236096 | bytes 7372800 | tf_op jit(solution)/shard_map/rj,rk->jk/dot_general | solution.py:84
  224.5 5.2 %copy.19 = bf16[1152,1152]{1,0:T(8,128)(2,1)} copy(bf16[1152,1152]{0,1:T(8,128)(2,1)} %fusion) | data formatting | bytes 5308416 | tf_op jit(solution)/shard_map/convert_element_type | solution.py:114
  229.8 3.6 reshape_reshape.6
  233.4 8.3 %pad_maximum_fusion = bf16[16,248832]{1,0:T(8,128)(2,1)} fusion(bf16[16,165888]{1,0:T(8,128)(2,1)} %reshape_reshape.7, bf16[16,82944]{1,0:T(8,128)(2,1)} %reshape_reshape.6), kind=kLoop, calls=%fused_computation.1 | loop fusion | flops 15925248 | bytes 15925248 | tf_op jit(solution)/shard_map/concatenate | solution.py:30
  241.7 7.6 %reshape.82 = bf16[31104,128]{1,0:T(8,128)(2,1)} reshape(bf16[16,248832]{1,0:T(8,128)(2,1)} %pad_maximum_fusion) | data formatting | bytes 15925248 | tf_op jit(solution)/shard_map/reshape | solution.py:32
  251.2 7.4 %convolution_convert_fusion.3 = bf16[1024,1152]{1,0:T(8,128)(2,1)} fusion(bf16[1024,1152]{1,0:T(8,128)(2,1)} %collective-permute-done.1, bf16[1,1152,1152]{2,1,0:T(8,128)(2,1)} %all-gather.3.cloned.1.call-done), kind=kOutput, calls=%fused_computation.18 | convolution fusion | flops 2719088640 | bytes 7372800 | tf_op jit(solution)/shard_map/rk,jk->rj/dot_general | solution.py:81
  258.7 151.7 %all-reduce.3.cloned.1.call-done = bf16[31104,128]{1,0:T(8,128)(2,1)} async-done(((bf16[31104,128]{1,0:T(8,128)(2,1)}), bf16[31104,128]{1,0:T(8,128)(2,1)}) %all-reduce.3.cloned.1.call-update) | async-done | bytes 7962640
  410.3 1.7 dynamic-slice_convert_fusion.1
  412.0 1.8 reshape.84
  413.8 1.9 dynamic-slice_convert_fusion
  415.6 2.1 reshape.85
  417.7 2.3 multiply_subtract_fusion.1
  419.9 3.0 multiply_subtract_fusion
  (22 shorter events, 4.4 us)
Async XLA Ops:
  7.2 56.6 %copy-start = (bf16[1,2,512,1152]{3,2,1,0:T(8,128)(2,1)S(1)}, bf16[1,2,512,1152]{3,2,1,0:T(8,128)(2,1)}, u32[]{:S(2)}) copy-start(bf16[1,2,512,1152]{3,2,1,0:T(8,128)(2,1)} %param.9) | copy-start | bytes 7077892
  7.2 56.6 %all-gather.3.cloned.1.call-start = ((), (), s32[]{:S(2)}) async-start(), calls=%async_computation | async-start | bytes 2820096 | tf_op jit(solution)/shard_map/all_gather | solution.py:91
  9.1 133.1 %all-gather.5.cloned.1.call-start = ((), (), s32[]{:S(2)}) async-start(), calls=%async_computation.1 | async-start | bytes 5640192 | tf_op jit(solution)/shard_map/all_gather | solution.py:92
  11.0 399.3 %all-reduce.3.cloned.1.call-start = ((), (), s32[]{:S(2)}) async-start(), calls=%async_computation.2 | async-start | bytes 15925248
  69.2 71.3 %collective-permute-start = (bf16[1024,1152]{1,0:T(8,128)(2,1)S(1)}, bf16[1024,1152]{1,0:T(8,128)(2,1)}, u32[]{:S(2)}, u32[]{:S(2)}) collective-permute-start(bf16[1024,1152]{1,0:T(8,128)(2,1)S(1)} %convolution_convert_fusion.4), channel_id=1, source_target_pairs={{0,64},{16,80},{32,96},{48,112},{64,0},{80,16},{96,32},{112,48},{1... | collective-permute-start | bytes 7077896 | tf_op jit(solution)/shard_map/ppermute | solution.py:19
  142.1 13.2 %copy-start.3 = (bf16[1,2304,1152]{2,1,0:T(8,128)(2,1)S(1)}, bf16[1,2304,1152]{2,1,0:T(8,128)(2,1)}, u32[]{:S(2)}) copy-start(bf16[1,2304,1152]{2,1,0:T(8,128)(2,1)} %all-gather.5.cloned.1.call-done) | copy-start | bytes 15925252
  161.9 3.2 copy-start.4
  164.4 53.7 %collective-permute-start.1 = (bf16[1024,1152]{1,0:T(8,128)(2,1)}, bf16[1024,1152]{1,0:T(8,128)(2,1)}, u32[]{:S(2)}, u32[]{:S(2)}) collective-permute-start(bf16[1024,1152]{1,0:T(8,128)(2,1)} %get-tuple-element.16), channel_id=1, source_target_pairs={{0,64},{16,80},{32,96},{48,112},{64,0},{80,16},{96,32},{112,48},{1... | collective-permute-start | bytes 7077896 | tf_op jit(solution)/shard_map/ppermute | solution.py:19
  249.3 0.7 copy-start.5
  251.2 166.5 %copy-start.2 = (f32[1,72,1152]{2,1,0:T(8,128)S(1)}, f32[1,72,1152]{2,1,0:T(8,128)}, u32[]{:S(2)}) copy-start(f32[1,72,1152]{2,1,0:T(8,128)} %param.12) | copy-start | bytes 995332
  258.7 161.3 %copy-start.1 = (f32[1,144,1152]{2,1,0:T(8,128)S(1)}, f32[1,144,1152]{2,1,0:T(8,128)}, u32[]{:S(2)}) copy-start(f32[1,144,1152]{2,1,0:T(8,128)} %param.13) | copy-start | bytes 1990660
Sparse Core Ops, SparseCore 0:
  11.0 52.6 all-gather.2
  66.7 75.4 all-gather.4
  249.5 160.8 all-reduce.2
where the time goes:
time: 430 us
  waiting for transfers between devices  316 us (73%)
  matrix products  47.4 us (11%)
  local copies, waits for them, and re-layouts  29.8 us (7%)
  other arithmetic  20.8 us (5%)
  between operations  14.5 us (3%)
    unnamed x4, waiting for transfers between devices  152 us
    ppermute x2, waiting for transfers between devices, swapped(): return lax.ppermute(value, axis, pairs)  110 us
    all_gather x1, waiting for transfers between devices, body(): lax.all_gather(w_proj.astype(jnp.bfloat16), 'dp', axis=1, tiled=True)  52.7 us
    dot_general x1, matrix products, layer_pass(): preact = jnp.dot(joined, skip_full, preferred_element_type=jnp.float32)  13.2 us
    another operation x2, local copies, waits for them, and re-layouts, one_scatter(): lines = jnp.concatenate([b.reshape(count, -1) for b in pieces], axis=1)  9.3 us
  transfers between devices with their start and end apart: 5, of which 5 were waited for; matrix products, arithmetic and copies ran while one was open for 7% of the time, Pallas kernels for 0%

commit v1 on v0

--- a/solution.py
+++ b/solution.py
@@ -88,7 +88,15 @@
 
 def body(enc_in, dec_in, cotangent, w_proj, w_skip, m_proj, v_proj, m_skip, v_skip):
     proj_all, skip_all = (
-        lax.all_gather(w_proj.astype(jnp.bfloat16), "dp", axis=1, tiled=True),
+        jnp.concatenate(
+            lax.all_to_all(
+                jnp.stack(lax.axis_size("dp") * [w_proj.astype(jnp.bfloat16)], 0),
+                axis_name="dp",
+                split_axis=0,
+                concat_axis=0,
+            ),
+            1,
+        ),
         lax.all_gather(w_skip.astype(jnp.bfloat16), "dp", axis=1, tiled=True),
     )
     proj_full = proj_all[0]

time: 430 us -> 416 us (0.967)
  waiting for transfers between devices: 316 us -> 256 us
  blocking collectives: 0 us -> 48.3 us
    all_gather x1 -> x0, waiting for transfers between devices: 52.7 us -> none  [body(): lax.all_gather(w_proj.astype(jnp.bfloat16), 'dp', axis=1, tiled=True)]
    all_to_all x0 -> x1, blocking collectives: none -> 48.3 us  [body(): lax.all_to_all(jnp.stack(lax.axis_size('dp') * [w_proj.astype(jnp.bfloat1...]
    ppermute x2, waiting for transfers between devices: 110 us -> 104 us  [swapped(): return lax.ppermute(value, axis, pairs)]
    unnamed x4 -> x3, waiting for transfers between devices: 152 us -> 152 us
  transfers between devices with their start and end apart: 5 -> 4, of which waited for: 5 -> 3; matrix products, arithmetic and copies ran while one was open for 7% -> 7% of each run, Pallas kernels for 0% -> 0%
where the time goes in v1:
time: 416 us; the launch traced here: 415 us
  waiting for transfers between devices  256 us (62%)
  blocking collectives  48.3 us (12%)
  matrix products  45 us (11%)
  local copies, waits for them, and re-layouts  30 us (7%)
  other arithmetic  20.1 us (5%)
  between operations  14.8 us (4%)
    unnamed x3, waiting for transfers between devices  152 us
    ppermute x2, waiting for transfers between devices, swapped(): return lax.ppermute(value, axis, pairs)  104 us
    all_to_all x1, blocking collectives, body(): lax.all_to_all(jnp.stack(lax.axis_size('dp') * [w_proj.astype(jnp.bfloat1...  48.3 us
    dot_general x1, matrix products, layer_pass(): preact = jnp.dot(joined, skip_full, preferred_element_type=jnp.float32)  12.6 us
    another operation x2, local copies, waits for them, and re-layouts, one_scatter(): lines = jnp.concatenate([b.reshape(count, -1) for b in pieces], axis=1)  9.31 us
    dot_general x1, matrix products, layer_pass(): jnp.einsum('rj,rk->jk', joined, pre_grad, preferred_element_type=jnp.floa...  8.36 us
  transfers between devices with their start and end apart: 4, of which 3 were waited for; matrix products, arithmetic and copies ran while one was open for 7% of the time, Pallas kernels for 0%

profile of v1, /device:TPU:0, one launch (start us, length us, event | category | flops | bytes accessed | tf_op | source)
XLA Modules:
  0.0 415.1 jit_solution(13920154905683651702)
XLA Ops:
  7.2 2.0 convert_element_type.76
  10.5 48.3 %all_to_all.5 = bf16[16,1,72,1152]{3,2,1,0:T(8,128)(2,1)S(1)} all-to-all(bf16[16,1,72,1152]{3,2,1,0:T(8,128)(2,1)S(1)} %stack.2), channel_id=1, replica_groups=mesh['section'=8,'dp'=16] {'dp'}, dimensions={0} | all-to-all | bytes 5308416 | tf_op jit(solution)/shard_map/all_to_all | solution.py:92
  58.8 3.7 convolution_convert_fusion.4
  62.5 1.1 collective-permute-start
  63.6 64.8 %collective-permute-done = bf16[1024,1152]{1,0:T(8,128)(2,1)} collective-permute-done((bf16[1024,1152]{1,0:T(8,128)(2,1)S(1)}, bf16[1024,1152]{1,0:T(8,128)(2,1)}, u32[]{:S(2)}, u32[]{:S(2)}) %collective-permute-start) | collective-permute-done | bytes 2359328 | tf_op jit(solution)/shard_map/ppermute | solution.py:19
  128.4 12.6 %fusion.9 = (bf16[1024,1152]{1,0:T(8,128)(2,1)S(1)}, bf16[1024,1152]{1,0:T(8,128)(2,1)}) fusion(bf16[1,2,512,1152]{3,2,1,0:T(8,128)(2,1)} %param.11, bf16[1,2304,1152]{2,1,0:T(8,128)(2,1)} %all-gather.2.cloned.1.call-done, bf16[1024,1152]{1,0:T(8,128)(2,1)} %collective-permute-done, bf16[1024,1152]{1,0:T(8,128)(2,1)} %bitcast.34), kind=kOutput, calls=%fused_computation.14 | convolution fusion | flops 5460590592 | bytes 17104896 | tf_op jit(solution)/shard_map/dot_general | solution.py:73
  141.0 6.5 %convolution_convert_fusion.2 = bf16[1024,2304]{1,0:T(8,128)(2,1)S(1)} fusion(bf16[1024,1152]{1,0:T(8,128)(2,1)S(1)} %get-tuple-element.17, bf16[1,2304,1152]{2,1,0:T(8,128)(2,1)S(1)} %copy-done.4), kind=kOutput, calls=%fused_computation.5 | convolution fusion | flops 5438177280 | bytes 12386304 | tf_op jit(solution)/shard_map/rk,jk->rj/dot_general | solution.py:77
  147.5 2.5 fusion.16
  150.3 8.4 %convolution_convert_fusion = bf16[2304,1152]{1,0:T(8,128)(2,1)} fusion(bf16[1024,1152]{1,0:T(8,128)(2,1)S(1)} %get-tuple-element.17, bf16[1024,1152]{1,0:T(8,128)(2,1)} %collective-permute-done, bf16[1024,1152]{1,0:T(8,128)(2,1)S(1)} %bitcast.35), kind=kOutput, calls=%fused_computation | convolution fusion | flops 5447909376 | bytes 12386304 | tf_op jit(solution)/shard_map/rj,rk->jk/dot_general | solution.py:85
  158.7 5.7 %reshape_reshape.7 = bf16[16,165888]{1,0:T(8,128)(2,1)} reshape(bf16[2304,1152]{1,0:T(8,128)(2,1)} %convolution_convert_fusion) | data formatting | bytes 10616832 | tf_op jit(solution)/shard_map/reshape;reshape | solution.py:30
  164.4 39.0 %collective-permute-done.1 = bf16[1024,1152]{1,0:T(8,128)(2,1)} collective-permute-done((bf16[1024,1152]{1,0:T(8,128)(2,1)}, bf16[1024,1152]{1,0:T(8,128)(2,1)}, u32[]{:S(2)}, u32[]{:S(2)}) %collective-permute-start.1) | collective-permute-done | bytes 2359328 | tf_op jit(solution)/shard_map/ppermute | solution.py:19
  203.4 6.4 %fusion = bf16[1152,1152]{0,1:T(8,128)(2,1)} fusion(bf16[1024,1152]{1,0:T(8,128)(2,1)} %collective-permute-done.1, bf16[1024,1152]{1,0:T(8,128)(2,1)S(1)} %bitcast.30), kind=kOutput, calls=%fused_computation.4 | convolution fusion | flops 2719236096 | bytes 7372800 | tf_op jit(solution)/shard_map/rj,rk->jk/dot_general | solution.py:84
  209.8 5.2 %copy.19 = bf16[1152,1152]{1,0:T(8,128)(2,1)} copy(bf16[1152,1152]{0,1:T(8,128)(2,1)} %fusion) | data formatting | bytes 5308416 | tf_op jit(solution)/shard_map/convert_element_type | solution.py:122
  215.0 3.6 reshape_reshape.6
  218.6 8.3 %pad_maximum_fusion = bf16[16,248832]{1,0:T(8,128)(2,1)} fusion(bf16[16,165888]{1,0:T(8,128)(2,1)} %reshape_reshape.7, bf16[16,82944]{1,0:T(8,128)(2,1)} %reshape_reshape.6), kind=kLoop, calls=%fused_computation.1 | loop fusion | flops 15925248 | bytes 15925248 | tf_op jit(solution)/shard_map/concatenate | solution.py:30
  226.9 7.6 %reshape.85 = bf16[31104,128]{1,0:T(8,128)(2,1)} reshape(bf16[16,248832]{1,0:T(8,128)(2,1)} %pad_maximum_fusion) | data formatting | bytes 15925248 | tf_op jit(solution)/shard_map/reshape | solution.py:32
  236.5 7.4 %convolution_convert_fusion.3 = bf16[1024,1152]{1,0:T(8,128)(2,1)} fusion(bf16[1024,1152]{1,0:T(8,128)(2,1)} %collective-permute-done.1, bf16[1152,1152]{1,0:T(8,128)(2,1)} %bitcast.32), kind=kOutput, calls=%fused_computation.18 | convolution fusion | flops 2719088640 | bytes 7372800 | tf_op jit(solution)/shard_map/rk,jk->rj/dot_general | solution.py:81
  243.9 151.7 %all-reduce.3.cloned.1.call-done = bf16[31104,128]{1,0:T(8,128)(2,1)} async-done(((bf16[31104,128]{1,0:T(8,128)(2,1)}), bf16[31104,128]{1,0:T(8,128)(2,1)}) %all-reduce.3.cloned.1.call-update) | async-done | bytes 7962640
  395.6 1.7 dynamic-slice_convert_fusion.1
  397.3 1.8 reshape.87
  399.1 1.9 dynamic-slice_convert_fusion
  401.0 2.1 reshape.88
  403.0 2.3 multiply_subtract_fusion.1
  405.3 3.0 multiply_subtract_fusion
  (23 shorter events, 2.8 us)
Async XLA Ops:
  7.2 51.6 %copy-start = (bf16[1,2,512,1152]{3,2,1,0:T(8,128)(2,1)S(1)}, bf16[1,2,512,1152]{3,2,1,0:T(8,128)(2,1)}, u32[]{:S(2)}) copy-start(bf16[1,2,512,1152]{3,2,1,0:T(8,128)(2,1)} %param.9) | copy-start | bytes 7077892
  7.2 121.2 %all-gather.2.cloned.1.call-start = ((), (), s32[]{:S(2)}) async-start(), calls=%async_computation.1 | async-start | bytes 5640192 | tf_op jit(solution)/shard_map/all_gather | solution.py:100
  9.3 386.4 %all-reduce.3.cloned.1.call-start = ((), (), s32[]{:S(2)}) async-start(), calls=%async_computation.2 | async-start | bytes 15925248
  58.8 3.8 copy-start.2
  62.5 65.9 %collective-permute-start = (bf16[1024,1152]{1,0:T(8,128)(2,1)S(1)}, bf16[1024,1152]{1,0:T(8,128)(2,1)}, u32[]{:S(2)}, u32[]{:S(2)}) collective-permute-start(bf16[1024,1152]{1,0:T(8,128)(2,1)S(1)} %convolution_convert_fusion.4), channel_id=1, source_target_pairs={{0,64},{16,80},{32,96},{48,112},{64,0},{80,16},{96,32},{112,48},{1... | collective-permute-start | bytes 7077896 | tf_op jit(solution)/shard_map/ppermute | solution.py:19
  128.4 12.6 %copy-start.4 = (bf16[1,2304,1152]{2,1,0:T(8,128)(2,1)S(1)}, bf16[1,2304,1152]{2,1,0:T(8,128)(2,1)}, u32[]{:S(2)}) copy-start(bf16[1,2304,1152]{2,1,0:T(8,128)(2,1)} %all-gather.2.cloned.1.call-done) | copy-start | bytes 15925252
  147.5 2.8 copy-start.5
  150.0 53.3 %collective-permute-start.1 = (bf16[1024,1152]{1,0:T(8,128)(2,1)}, bf16[1024,1152]{1,0:T(8,128)(2,1)}, u32[]{:S(2)}, u32[]{:S(2)}) collective-permute-start(bf16[1024,1152]{1,0:T(8,128)(2,1)} %get-tuple-element.16), channel_id=1, source_target_pairs={{0,64},{16,80},{32,96},{48,112},{64,0},{80,16},{96,32},{112,48},{1... | collective-permute-start | bytes 7077896 | tf_op jit(solution)/shard_map/ppermute | solution.py:19
  234.6 0.7 copy-start.6
  236.5 166.6 %copy-start.3 = (f32[1,72,1152]{2,1,0:T(8,128)S(1)}, f32[1,72,1152]{2,1,0:T(8,128)}, u32[]{:S(2)}) copy-start(f32[1,72,1152]{2,1,0:T(8,128)} %param.12) | copy-start | bytes 995332
  243.9 161.4 %copy-start.1 = (f32[1,144,1152]{2,1,0:T(8,128)S(1)}, f32[1,144,1152]{2,1,0:T(8,128)}, u32[]{:S(2)}) copy-start(f32[1,144,1152]{2,1,0:T(8,128)} %param.13) | copy-start | bytes 1990660
Sparse Core Ops, SparseCore 0:
  10.9 92.7 all-gather.1
  234.7 160.8 all-reduce.2
